TPU v7x, 32 devices: a whole 2x2x4 slice. The times are simulated.
32 devices in a mesh: grp: 4 (over z), mem: 8 (over y, x, core).
Axes of the slice: x: 2, y: 2, z: 4, core: 2. Of those that a mesh axis runs over, the one named last changes fastest.
Arguments:
- volume: float32 [4, 8, 8, 512, 1024], P('grp', 'mem'), may hold values from -1 to 1
- transfer_coef: float32 [4, 4], replicated, may hold values from -3 to 3
- group_order: int32 [4], replicated, may hold values from 0 to 3, each once
- member_order: int32 [4, 8], replicated, may hold values from 0 to 7, each once within a row
- active_mask: int32 [4, 8], P('grp', 'mem'), may hold values 0 or 1
Outputs:
- picture: float32 [4, 512, 1024], P(None, 'mem', 'grp')
All inputs are finite; a program needn't handle non-finite values. No bound on the sum of `active_mask` on one device may be relied on, other than what follows from the above.
Results may differ from a plain program's by a relative error of at most 0.0003.
Values sent between devices are 32-bit elements; how exact they have to be, the bound alone decides.
A program may use at most 192 MiB of HBM per device.

v0:
```python
import jax
import jax.numpy as jnp
from jax import lax
from jax.sharding import PartitionSpec as P


def polynomial(coef_row, values):
    return coef_row[0] + values * (coef_row[1] + values * (coef_row[2] + values * coef_row[3]))


def march_brick(samples, transfer_coef, active_flag, density_scale):
    optical_depth = jnp.zeros(samples.shape[1:], jnp.float32)
    colour = jnp.zeros((3,) + samples.shape[1:], jnp.float32)
    for sample_index in range(samples.shape[0]):
        values = samples[sample_index]
        extinction = polynomial(transfer_coef[3], values) ** 2 * density_scale
        opacity = 1.0 - jnp.exp(-extinction)
        tinted = jax.nn.sigmoid(
            jnp.stack([polynomial(transfer_coef[channel], values) for channel in range(3)])
        )
        colour = colour + (jnp.exp(-optical_depth) * opacity)[None] * tinted
        optical_depth = optical_depth + extinction
    coverage = 1.0 - jnp.exp(-optical_depth)
    return jnp.concatenate([colour, coverage[None]], 0) * active_flag


def reorder(layers, rank_list):
    total = rank_list.shape[0]
    positions = jnp.arange(total, dtype=jnp.int32)
    inverse = jnp.sum(
        positions[:, None] * (rank_list[:, None] == positions[None, :]).astype(jnp.int32), axis=0
    )
    return jnp.take(layers, inverse, axis=0)


def over_tree(layers):
    while layers.shape[0] > 1:
        nearer = layers[0::2]
        farther = layers[1::2]
        layers = nearer + (1.0 - nearer[:, 3:4]) * farther
    return layers[0]


def body(volume, transfer_coef, group_order, member_order, active_mask):
    groups = lax.axis_size("grp")
    members = lax.axis_size("mem")
    density_scale = 3.0 / (volume.shape[2] * groups * members)
    active_flag = active_mask[0, 0].astype(jnp.float32)
    layer = march_brick(volume[0, 0], transfer_coef, active_flag, density_scale)
    slab_ranks = lax.dynamic_slice_in_dim(member_order, lax.axis_index("grp"), 1, 0)[0]
    slab_image = over_tree(
        reorder(
            lax.all_to_all(layer[None], "mem", split_axis=2, concat_axis=0, tiled=True), slab_ranks
        )
    )
    return over_tree(
        reorder(
            lax.all_to_all(slab_image[None], "grp", split_axis=3, concat_axis=0, tiled=True),
            group_order,
        )
    )


def solution(mesh):
    in_specs = (P("grp", "mem", None, None, None), P(), P(), P(), P("grp", "mem"))
    out_specs = P(None, "mem", "grp")
    return jax.shard_map(body, mesh=mesh, in_specs=in_specs, out_specs=out_specs, check_vma=False)
```

profile of v0, /device:TPU:2, one launch (start us, length us, event | category | flops | bytes accessed | tf_op | source)
XLA Modules:
  0.0 448.7 jit_solution(17760567947958751179)
XLA Ops:
  0.0 0.0 copy-start
  0.0 0.0 copy-start.9
  0.0 6.7 %slice_bitcast_fusion = (f32[1,512,1024]{2,1,0:T(8,128)S(1)}, f32[1,1,1,512,1024]{4,3,2,1,0:T(8,128)S(1)}, f32[1,1,1,512,1024]{4,3,2,1,0:T(8,128)S(1)}, f32[1,1,...) fusion(f32[1,1,8,512,1024]{4,3,2,1,0:T(8,128)} %param.5), kind=kLoop, calls=%fused_computation.159 | loop fusion | bytes 33554432 | tf_op jit(solution)/shard_map/squeeze | solution.py:15
  6.7 0.0 copy-done.9
  6.7 0.0 copy-start.1
  6.7 0.9 fusion.105
  7.6 31.3 %multiply_add_fusion.4 = (f32[1,512,1024]{2,0,1:T(1,128)}, f32[1,512,1024]{2,0,1:T(1,128)}, f32[1,512,1024]{2,0,1:T(1,128)}, f32[1,512,1024]{2,0,1:T(1,128)}, f3...) fusion(f32[]{:T(128)} %bitcast.9, f32[]{:T(128)} %bitcast.8, f32[]{:T(128)} %bitcast.7, f32[]{:T(128)} %bitcast.6, ...), kind=kLoop, calls=%fused_computation.130 | loop fusion | flops 18874368 | bytes 16777264 | tf_op jit(solution)/shard_map/add | solution.py:8
  39.0 0.0 copy-done.1
  39.0 30.7 %multiply_add_fusion.10 = (f32[1,512,1024]{2,0,1:T(1,128)}, f32[1,512,1024]{2,0,1:T(1,128)}, f32[1,512,1024]{2,0,1:T(1,128)}, f32[1,512,1024]{2,0,1:T(1,128)}, f...) fusion(f32[1,1,1,512,1024]{4,3,2,1,0:T(8,128)S(1)} %get-tuple-element.16, f32[]{:T(128)} %bitcast.9, f32[]{:T(128)} %bitcast.8, ...), kind=kLoop, calls=%fused_computation.137 | loop fusion | flops 18874368 | bytes 16777264 | tf_op jit(solution)/shard_map/add | solution.py:8
  69.6 30.7 %multiply_add_fusion.16 = (f32[1,512,1024]{2,0,1:T(1,128)}, f32[1,512,1024]{2,0,1:T(1,128)}, f32[1,512,1024]{2,0,1:T(1,128)}, f32[1,512,1024]{2,0,1:T(1,128)}, f...) fusion(f32[1,1,1,512,1024]{4,3,2,1,0:T(8,128)S(1)} %get-tuple-element.18, f32[]{:T(128)} %bitcast.9, f32[]{:T(128)} %bitcast.8, ...), kind=kLoop, calls=%fused_computation.145 | loop fusion | flops 18874368 | bytes 16777264 | tf_op jit(solution)/shard_map/add | solution.py:8
  100.3 0.0 copy-start.2
  100.3 0.0 slice-start.1
  100.3 32.0 %multiply_add_fusion.22 = (f32[1,512,1024]{2,0,1:T(1,128)}, f32[1,512,1024]{2,0,1:T(1,128)}, f32[1,512,1024]{2,0,1:T(1,128)}, f32[1,512,1024]{2,0,1:T(1,128)}, f...) fusion(f32[1,1,1,512,1024]{4,3,2,1,0:T(8,128)S(1)} %get-tuple-element.20, f32[]{:T(128)} %bitcast.9, f32[]{:T(128)} %bitcast.8, ...), kind=kLoop, calls=%fused_computation.153 | loop fusion | flops 18874368 | bytes 16777264 | tf_op jit(solution)/shard_map/add | solution.py:8
  132.3 0.0 copy-done.2
  132.3 0.0 slice-start.2
  132.3 0.0 slice-start.3
  132.3 41.6 %fusion.86 = f32[1,1,512,1024]{3,1,0,2:T(1,128)} fusion(f32[1,1,1,512,1024]{4,3,2,1,0:T(8,128)S(1)} %get-tuple-element.16, f32[1,1,1,512,1024]{4,3,2,1,0:T(8,128)S(1)} %get-tuple-element.17, f32[1,1,1,512,1024]{4,3,2,1,0:T(8,128)S(1)} %get-tuple-element.18, f32[1,1,1,512,1024]{4,3,2,1,0:T(8,128)S(1)} %get-tuple-element.19, ...), kind=kLoop, calls=%fused_computation.126 | loop fusion | flops 34603008 | bytes 18874384 | tf_op jit(solution)/shard_map/concatenate | solution.py:24
  174.0 0.0 slice-done
  174.0 0.0 slice-done.1
  174.0 0.0 slice-done.2
  174.0 0.0 slice-done.3
  174.0 6.2 %subtract_multiply_fusion.3 = (f32[512,1024]{1,0:T(8,128)}, f32[512,1024]{1,0:T(8,128)S(1)}) fusion(f32[]{:T(128)} %bitcast.5, f32[]{:T(128)} %bitcast.4, f32[]{:T(128)} %bitcast.3, f32[]{:T(128)} %bitcast.1, f32[1,1,8,512,1024]{4,3,2,1,0:T(8,128)S(1)} %bitcast.282), kind=kLoop, calls=%fused_computation.146 | loop fusion | flops 19922944 | bytes 12582928 | tf_op jit(solution)/shard_map/mul | solution.py:21
  180.2 6.7 %subtract_multiply_fusion.1 = (f32[512,1024]{1,0:T(8,128)}, f32[512,1024]{1,0:T(8,128)S(1)}, f32[512,1024]{1,0:T(8,128)}) fusion(f32[]{:T(128)} %bitcast.5, f32[]{:T(128)} %bitcast.4, f32[]{:T(128)} %bitcast.3, f32[]{:T(128)} %bitcast.1, f32[1,1,8,512,1024]{4,3,2,1,0:T(8,128)S(1)} %bitcast.282, f32[512,1024]{1,0:T(8,128)S(1)} %get-tuple-element.6), kind=kLoop, calls=%fused_computation.138 | loop fusion | flops 17825792 | bytes 14680080 | tf_op jit(solution)/shard_map/mul | solution.py:21
  187.0 0.0 copy-start.3
  187.0 0.0 copy-start.4
  187.0 0.0 copy-start.7
  187.0 0.0 copy-start.8
  187.0 11.5 %subtract_multiply_fusion = (f32[512,1024]{1,0:T(8,128)}, f32[512,1024]{1,0:T(8,128)}, f32[512,1024]{1,0:T(8,128)}, f32[512,1024]{1,0:T(8,128)}, f32[512,1024]{1,0:T(8,128)}) fusion(f32[]{:T(128)} %bitcast.5, f32[]{:T(128)} %bitcast.4, f32[]{:T(128)} %bitcast.3, f32[]{:T(128)} %bitcast.1, f32[512,1024]{1,0:T(8,128)S(1)} %get-tuple-element.8, ...), kind=kLoop, calls=%fused_computation.134 | loop fusion | flops 35651584 | bytes 25165840 | tf_op jit(solution)/shard_map/mul | solution.py:21
  199.2 0.0 copy-done.3
  199.2 0.0 copy-done.4
  199.2 0.0 copy-done.5
  199.2 0.0 copy-done.6
  199.2 0.0 copy-done.7
  199.2 0.0 copy-done.8
  199.2 75.1 %fusion.39 = f32[1,3,512,1024]{3,1,0,2:T(4,128)S(1)} fusion(f32[1,512,1024]{2,0,1:T(1,128)S(1)} %copy-done.4, f32[1,512,1024]{2,0,1:T(1,128)S(1)} %copy-done.5, f32[1,512,1024]{2,0,1:T(1,128)S(1)} %copy-done.3, f32[1,512,1024]{2,0,1:T(1,128)S(1)} %copy-done.6, f32[1,512,1024]{2,0,1:T(1,128)S(1)} %copy-done.7, f32[1,512,1024]{2,0,1:T(1,128)S(1)} %copy-done.8, ...), kind=kLoop, calls=%fused_computation.51 | loop fusion | flops 86507520 | bytes 73400320 | tf_op jit(solution)/shard_map/concatenate | solution.py:24
  274.3 7.1 %maximum_multiply_fusion = f32[1,4,512,1024]{3,1,0,2:T(4,128)} fusion(f32[1,1,512,1024]{3,1,0,2:T(1,128)} %fusion.86, f32[1,3,512,1024]{3,1,0,2:T(4,128)S(1)} %fusion.39, f32[]{:T(128)} %bitcast.29), kind=kLoop, calls=%fused_computation.49 | loop fusion | flops 4194304 | bytes 16777220 | tf_op jit(solution)/shard_map/mul | solution.py:24
  281.4 5.1 %all-to-all-start = ((f32[1,4,512,1024]{3,1,0,2:T(4,128)}), f32[1,4,512,1024]{3,1,0,2:T(4,128)}, u32[]{:S(2)}, u32[]{:S(2)}) async-start(f32[1,4,512,1024]{3,1,0,2:T(4,128)} %maximum_multiply_fusion), calls=%async_computation | async-start | bytes 16777216 | tf_op jit(solution)/shard_map/all_to_all | solution.py:53
  286.5 0.0 copy-done
  286.5 0.1 select_reduce_fusion
  286.6 92.2 %all-to-all-done = f32[1,4,512,1024]{3,1,0,2:T(4,128)} async-done(((f32[1,4,512,1024]{3,1,0,2:T(4,128)}), f32[1,4,512,1024]{3,1,0,2:T(4,128)}, u32[]{:S(2)}, u32[]{:S(2)}) %all-to-all-start) | async-done | bytes 8388640 | tf_op jit(solution)/shard_map/all_to_all | solution.py:53
  378.8 11.3 %copy.99 = f32[1,4,8,64,1024]{4,3,1,2,0:T(8,128)} copy(f32[1,4,8,64,1024]{4,1,3,2,0:T(4,128)} %bitcast.30) | data formatting | bytes 16777216 | tf_op jit(solution)/shard_map/all_to_all | solution.py:53
  390.1 7.7 %gather_fusion = f32[8,4,64,1024]{3,2,1,0:T(8,128)} fusion(f32[8,4,64,1024]{3,2,1,0:T(8,128)} %bitcast.283, s32[1024]{0:T(1024)S(1)} %pad_clamp_fusion.1), kind=kCustom, calls=%fused_computation | custom fusion | bytes 16777248 | tf_op jit(solution)/shard_map/jit(_take)/gather | solution.py:33
  397.9 4.4 broadcast_select_fusion
  402.3 0.5 slice.148
  402.8 0.1 fusion.94
  402.9 1.1 multiply_add_fusion
  404.1 0.1 slice.151
  404.3 0.7 multiply_add_fusion.1
  405.0 0.2 fusion.93
  405.2 0.9 copy.75
  406.1 0.0 copy-start.10
  406.1 2.9 reshape.2041
  409.0 5.4 %all-to-all-start.1 = ((f32[4,1,65536]{2,1,0:T(1,128)}), f32[4,1,65536]{2,1,0:T(1,128)S(1)}, u32[]{:S(2)}, u32[]{:S(2)}) async-start(f32[4,1,65536]{2,1,0:T(1,128)} %reshape.2041), calls=%async_computation.1 | async-start | bytes 2097152 | tf_op jit(solution)/shard_map/all_to_all | solution.py:58
  414.5 0.0 copy-done.10
  414.5 0.1 select_reduce_fusion.1
  414.6 25.8 %all-to-all-done.1 = f32[4,1,65536]{2,1,0:T(1,128)S(1)} async-done(((f32[4,1,65536]{2,1,0:T(1,128)}), f32[4,1,65536]{2,1,0:T(1,128)S(1)}, u32[]{:S(2)}, u32[]{:S(2)}) %all-to-all-start.1) | async-done | bytes 1048608 | tf_op jit(solution)/shard_map/all_to_all | solution.py:58
  440.4 0.5 broadcast.2075
  441.0 3.8 reduce
  444.7 1.4 reshape.2042
  446.2 0.8 copy.77
  447.0 0.6 gather_fusion.1
  447.6 0.2 broadcast_select_fusion.1
  447.9 0.1 multiply_add_fusion.26
  448.0 0.7 fusion.97
  (16 shorter events, 0.2 us)
Async XLA Ops:
  0.0 286.5 %copy-start = (s32[4,8]{1,0:T(4,128)S(1)}, s32[4,8]{1,0:T(4,128)}, u32[]{:S(2)}) copy-start(s32[4,8]{1,0:T(4,128)} %param.8) | copy-start | bytes 388
  0.0 6.7 %copy-start.9 = (f32[4,4]{1,0:T(4,128)S(1)}, f32[4,4]{1,0:T(4,128)}, u32[]{:S(2)}) copy-start(f32[4,4]{1,0:T(4,128)} %param.6) | copy-start | bytes 196
  6.7 32.2 %copy-start.1 = (f32[1,1,1,512,1024]{4,3,2,1,0:T(8,128)}, f32[1,1,1,512,1024]{4,3,2,1,0:T(8,128)S(1)}, u32[]{:S(2)}) copy-start(f32[1,1,1,512,1024]{4,3,2,1,0:T(8,128)S(1)} %get-tuple-element.22) | copy-start | bytes 6291460
  100.3 32.0 %copy-start.2 = (f32[1,1,1,512,1024]{4,3,2,1,0:T(8,128)S(1)}, f32[1,1,1,512,1024]{4,3,2,1,0:T(8,128)}, u32[]{:S(2)}) copy-start(f32[1,1,1,512,1024]{4,3,2,1,0:T(8,128)} %copy-done.1) | copy-start | bytes 6291460
  100.3 73.6 %slice-start = ((s8[16777216]{0:T(1024)(128)(4,1)}), s8[4194304]{0:T(1024)(128)(4,1)S(1)}, s32[]{:S(2)}) async-start(s8[16777216]{0:T(1024)(128)(4,1)} %bitcast.281), calls=%async_computation.2 | async-start | bytes 8388608
  100.3 73.6 %slice-start.1 = ((s8[16777216]{0:T(1024)(128)(4,1)}), s8[4194304]{0:T(1024)(128)(4,1)S(1)}, s32[]{:S(2)}) async-start(s8[16777216]{0:T(1024)(128)(4,1)} %bitcast.281), calls=%async_computation.3 | async-start | bytes 8388608
  132.3 41.6 %slice-start.2 = ((s8[16777216]{0:T(1024)(128)(4,1)}), s8[4194304]{0:T(1024)(128)(4,1)S(1)}, s32[]{:S(2)}) async-start(s8[16777216]{0:T(1024)(128)(4,1)} %bitcast.281), calls=%async_computation.4 | async-start | bytes 8388608
  132.3 41.6 %slice-start.3 = ((s8[16777216]{0:T(1024)(128)(4,1)}), s8[4194304]{0:T(1024)(128)(4,1)S(1)}, s32[]{:S(2)}) async-start(s8[16777216]{0:T(1024)(128)(4,1)} %bitcast.281), calls=%async_computation.5 | async-start | bytes 8388608
  187.0 12.2 %copy-start.3 = (f32[1,512,1024]{2,0,1:T(1,128)S(1)}, f32[1,512,1024]{2,0,1:T(1,128)}, u32[]{:S(2)}) copy-start(f32[1,512,1024]{2,0,1:T(1,128)} %get-tuple-element.44) | copy-start | bytes 6291460
  187.0 12.2 %copy-start.4 = (f32[1,512,1024]{2,0,1:T(1,128)S(1)}, f32[1,512,1024]{2,0,1:T(1,128)}, u32[]{:S(2)}) copy-start(f32[1,512,1024]{2,0,1:T(1,128)} %get-tuple-element.45) | copy-start | bytes 6291460
  187.0 12.2 %copy-start.5 = (f32[1,512,1024]{2,0,1:T(1,128)S(1)}, f32[1,512,1024]{2,0,1:T(1,128)}, u32[]{:S(2)}) copy-start(f32[1,512,1024]{2,0,1:T(1,128)} %get-tuple-element.46) | copy-start | bytes 6291460
  187.0 12.2 %copy-start.6 = (f32[1,512,1024]{2,0,1:T(1,128)S(1)}, f32[1,512,1024]{2,0,1:T(1,128)}, u32[]{:S(2)}) copy-start(f32[1,512,1024]{2,0,1:T(1,128)} %get-tuple-element.63) | copy-start | bytes 6291460
  187.0 12.2 %copy-start.7 = (f32[1,512,1024]{2,0,1:T(1,128)S(1)}, f32[1,512,1024]{2,0,1:T(1,128)}, u32[]{:S(2)}) copy-start(f32[1,512,1024]{2,0,1:T(1,128)} %get-tuple-element.64) | copy-start | bytes 6291460
  187.0 12.2 %copy-start.8 = (f32[1,512,1024]{2,0,1:T(1,128)S(1)}, f32[1,512,1024]{2,0,1:T(1,128)}, u32[]{:S(2)}) copy-start(f32[1,512,1024]{2,0,1:T(1,128)} %get-tuple-element.65) | copy-start | bytes 6291460
  281.4 97.5 %all-to-all-start = ((f32[1,4,512,1024]{3,1,0,2:T(4,128)}), f32[1,4,512,1024]{3,1,0,2:T(4,128)}, u32[]{:S(2)}, u32[]{:S(2)}) async-start(f32[1,4,512,1024]{3,1,0,2:T(4,128)} %maximum_multiply_fusion), calls=%async_computation | async-start | bytes 16777216 | tf_op jit(solution)/shard_map/all_to_all | solution.py:53
  406.1 8.4 %copy-start.10 = (s32[4]{0:T(128)S(1)}, s32[4]{0:T(128)}, u32[]{:S(2)}) copy-start(s32[4]{0:T(128)} %param.7) | copy-start | bytes 52
  409.0 31.4 %all-to-all-start.1 = ((f32[4,1,65536]{2,1,0:T(1,128)}), f32[4,1,65536]{2,1,0:T(1,128)S(1)}, u32[]{:S(2)}, u32[]{:S(2)}) async-start(f32[4,1,65536]{2,1,0:T(1,128)} %reshape.2041), calls=%async_computation.1 | async-start | bytes 2097152 | tf_op jit(solution)/shard_map/all_to_all | solution.py:58
where the time goes:
time: 450 us; the launch traced here: 449 us
  other arithmetic  285 us (63%)
  waiting for transfers between devices  118 us (26%)
  local copies, waits for them, and re-layouts  34.6 us (8%)
  starting transfers between devices  10.6 us (2%)
    add x4, other arithmetic, polynomial(): coef_row[0]  125 us
    concatenate x2, other arithmetic, march_brick(): return jnp.concatenate([colour, coverage[None]], 0) * active_flag  117 us
    all_to_all x1, waiting for transfers between devices, body(): lax.all_to_all(layer[None], 'mem', split_axis=2, concat_axis=0, tiled=True)  92.2 us
    all_to_all x1, waiting for transfers between devices, body(): lax.all_to_all(slab_image[None], 'grp', split_axis=3, concat_axis=0, tile...  25.8 us
    mul x3, other arithmetic, march_brick(): colour = colour + (jnp.exp(-optical_depth) * opacity)[None] * tinted  24.5 us
    all_to_all x1, local copies, waits for them, and re-layouts, body(): lax.all_to_all(layer[None], 'mem', split_axis=2, concat_axis=0, tiled=True)  11.3 us
  transfers between devices with their start and end apart: 2, of which 2 were waited for; matrix products, arithmetic and copies ran while one was open for 0% of the time, Pallas kernels for 0%

commit v1 on v0

--- a/solution.py
+++ b/solution.py
@@ -1,7 +1,39 @@
+import functools
 import jax
 import jax.numpy as jnp
 from jax import lax
 from jax.sharding import PartitionSpec as P
+
+
+def draw_cubes_all(array_here, d0, u):
+    view_out = array_here.shape
+    r1 = array_here.reshape(*view_out[:d0], u, view_out[d0] // u, *view_out[d0 + 1 :])
+    return jnp.moveaxis(r1, d0, 0)
+
+
+def sources_all_close(packet, axis_k):
+    front = list(packet.shape[1:])
+    front[axis_k] *= packet.shape[0]
+    return jnp.moveaxis(packet, 0, axis_k).reshape(front)
+
+
+def table_solve(z, which_axis, frame_in, xin):
+    local_out, tmp = (lax.axis_size(which_axis), lax.axis_index(which_axis))
+    earlier = draw_cubes_all(z, frame_in, local_out)
+    outcome_arr = earlier
+    for k in range(1, local_out):
+        d_next, arr_out = ((tmp + k) % local_out, (tmp - k) % local_out)
+        a_next = lax.dynamic_index_in_dim(earlier, d_next, 0)
+        e_now = lax.ppermute(
+            a_next,
+            axis_name=which_axis,
+            perm=list(map(lambda ix: (ix, (ix + k) % local_out), range(local_out))),
+        )
+        outcome_arr = lax.dynamic_update_slice_in_dim(outcome_arr, e_now, arr_out, axis=0)
+    return sources_all_close(outcome_arr, xin)
+
+
+lead_files_by_axis = functools.partial(table_solve, which_axis="mem", frame_in=2, xin=0)
 
 
 def polynomial(coef_row, values):
@@ -48,11 +80,7 @@
     active_flag = active_mask[0, 0].astype(jnp.float32)
     layer = march_brick(volume[0, 0], transfer_coef, active_flag, density_scale)
     slab_ranks = lax.dynamic_slice_in_dim(member_order, lax.axis_index("grp"), 1, 0)[0]
-    slab_image = over_tree(
-        reorder(
-            lax.all_to_all(layer[None], "mem", split_axis=2, concat_axis=0, tiled=True), slab_ranks
-        )
-    )
+    slab_image = over_tree(reorder(lead_files_by_axis(layer[None]), slab_ranks))
     return over_tree(
         reorder(
             lax.all_to_all(slab_image[None], "grp", split_axis=3, concat_axis=0, tiled=True),

time: 450 us -> 277 us (0.62)
  other arithmetic: 285 us -> 143 us
  waiting for transfers between devices: 118 us -> 65.7 us
  starting transfers between devices: 10.6 us -> 25.3 us
  local copies, waits for them, and re-layouts: 34.6 us -> 40.5 us
    concatenate x2 -> x1, other arithmetic: 117 us -> 11.8 us  [march_brick(): return jnp.concatenate([colour, coverage[None]], 0) * active_flag]
    all_to_all x1 -> x0, waiting for transfers between devices: 92.2 us -> none  [body(): lax.all_to_all(layer[None], 'mem', split_axis=2, concat_axis=0, tiled=True)]
    add x4, other arithmetic: 125 us -> 51.1 us  [polynomial(): coef_row[0]]
    ppermute x0 -> x7, waiting for transfers between devices: none -> 38.8 us  [table_solve(): lax.ppermute(a_next, axis_name=which_axis, perm=list(map(lambda ix: (ix,...]
    reshape x0 -> x1, other arithmetic: none -> 24.5 us  [sources_all_close(): return jnp.moveaxis(packet, 0, axis_k).reshape(front)]
    ppermute x0 -> x7, starting transfers between devices: none -> 20.4 us  [table_solve(): lax.ppermute(a_next, axis_name=which_axis, perm=list(map(lambda ix: (ix,...]
    mul x1, other arithmetic: 7.07 us -> 21.7 us  [march_brick(): return jnp.concatenate([colour, coverage[None]], 0) * active_flag]
    dynamic_update_slice x0 -> x7, local copies, waits for them, and re-layouts: none -> 13.8 us  [table_solve(): lax.dynamic_update_slice_in_dim(outcome_arr, e_now, arr_out, axis=0)]
  transfers between devices with their start and end apart: 2 -> 8, of which waited for: 2 -> 2; matrix products, arithmetic and copies ran while one was open for 0% -> 14% of each run, Pallas kernels for 0% -> 0%
where the time goes in v1:
time: 277 us; the launch traced here: 276 us
  other arithmetic  143 us (52%)
  waiting for transfers between devices  65.7 us (24%)
  local copies, waits for them, and re-layouts  40.5 us (15%)
  starting transfers between devices  25.3 us (9%)
    add x4, other arithmetic, polynomial(): coef_row[0]  51.1 us
    ppermute x7, waiting for transfers between devices, table_solve(): lax.ppermute(a_next, axis_name=which_axis, perm=list(map(lambda ix: (ix,...  38.8 us
    all_to_all x1, waiting for transfers between devices, body(): lax.all_to_all(slab_image[None], 'grp', split_axis=3, concat_axis=0, tile...  26.9 us
    reshape x1, other arithmetic, sources_all_close(): return jnp.moveaxis(packet, 0, axis_k).reshape(front)  24.5 us
    mul x3, other arithmetic, march_brick(): colour = colour + (jnp.exp(-optical_depth) * opacity)[None] * tinted  22.2 us
    mul x1, other arithmetic, march_brick(): return jnp.concatenate([colour, coverage[None]], 0) * active_flag  21.7 us
    ppermute x7, starting transfers between devices, table_solve(): lax.ppermute(a_next, axis_name=which_axis, perm=list(map(lambda ix: (ix,...  20.4 us
    dynamic_update_slice x7, local copies, waits for them, and re-layouts, table_solve(): lax.dynamic_update_slice_in_dim(outcome_arr, e_now, arr_out, axis=0)  13.8 us
  transfers between devices with their start and end apart: 8, of which 2 were waited for; matrix products, arithmetic and copies ran while one was open for 14% of the time, Pallas kernels for 0%

profile of v1, /device:TPU:2, one launch (start us, length us, event | category | flops | bytes accessed | tf_op | source)
XLA Modules:
  0.0 275.6 jit_solution(9909815992452212457)
XLA Ops:
  0.0 0.0 copy-start
  0.7 6.7 %fusion.62 = (f32[1,1,1,512,1024]{4,3,2,1,0:T(8,128)S(1)}, f32[1,1,1,512,1024]{4,3,2,1,0:T(8,128)S(1)}, f32[1,1,1,512,1024]{4,3,2,1,0:T(8,128)S(1)}, f32[1,1,1,5...) fusion(f32[1,1,8,512,1024]{4,3,2,1,0:T(8,128)} %param.5), kind=kLoop, calls=%fused_computation.150 | loop fusion | bytes 33554432 | tf_op jit(solution)/shard_map/slice | solution.py:47
  7.5 1.0 fusion.63
  8.4 12.8 %multiply_add_fusion.4 = (f32[1,8,64,1024]{3,2,1,0:T(8,128)}, f32[1,8,64,1024]{3,2,1,0:T(8,128)}, f32[1,8,64,1024]{3,2,1,0:T(8,128)}, f32[1,8,64,1024]{3,2,1,0:T...) fusion(f32[1,8,64,1024]{3,2,1,0:T(8,128)S(1)} %bitcast.118, f32[]{:T(128)} %bitcast.10, f32[]{:T(128)} %bitcast.9, ...), kind=kLoop, calls=%fused_computation.60 | loop fusion | flops 18874368 | bytes 16777264 | tf_op jit(solution)/shard_map/add | solution.py:40
  21.3 0.0 copy-done.1
  21.3 0.0 copy-done.13
  21.3 12.8 %multiply_add_fusion.10 = (f32[1,8,64,1024]{3,2,1,0:T(8,128)}, f32[1,8,64,1024]{3,2,1,0:T(8,128)}, f32[1,8,64,1024]{3,2,1,0:T(8,128)}, f32[1,8,64,1024]{3,2,1,0:...) fusion(f32[1,8,64,1024]{3,2,1,0:T(8,128)S(1)} %bitcast.105, f32[]{:T(128)} %bitcast.10, f32[]{:T(128)} %bitcast.9, ...), kind=kLoop, calls=%fused_computation.69 | loop fusion | flops 18874368 | bytes 16777264 | tf_op jit(solution)/shard_map/add | solution.py:40
  34.1 12.8 %multiply_add_fusion.16 = (f32[1,8,64,1024]{3,2,1,0:T(8,128)}, f32[1,8,64,1024]{3,2,1,0:T(8,128)}, f32[1,8,64,1024]{3,2,1,0:T(8,128)}, f32[1,8,64,1024]{3,2,1,0:...) fusion(f32[1,8,64,1024]{3,2,1,0:T(8,128)S(1)} %bitcast.101, f32[]{:T(128)} %bitcast.10, f32[]{:T(128)} %bitcast.9, ...), kind=kLoop, calls=%fused_computation.79 | loop fusion | flops 18874368 | bytes 16777264 | tf_op jit(solution)/shard_map/add | solution.py:40
  46.9 0.0 copy-done.7
  46.9 12.7 %multiply_add_fusion.22 = (f32[1,8,64,1024]{3,2,1,0:T(8,128)}, f32[1,8,64,1024]{3,2,1,0:T(8,128)}, f32[1,8,64,1024]{3,2,1,0:T(8,128)}, f32[1,8,64,1024]{3,2,1,0:...) fusion(f32[1,8,64,1024]{3,2,1,0:T(8,128)S(1)} %bitcast.115, f32[]{:T(128)} %bitcast.10, f32[]{:T(128)} %bitcast.9, ...), kind=kLoop, calls=%fused_computation.89 | loop fusion | flops 18874368 | bytes 16777264 | tf_op jit(solution)/shard_map/add | solution.py:40
  59.6 11.8 %fusion.42 = f32[1,1,8,64,1024]{4,3,1,2,0:T(8,128)} fusion(f32[1,8,64,1024]{3,2,1,0:T(8,128)} %bitcast.119, f32[1,8,64,1024]{3,2,1,0:T(8,128)} %bitcast.122, f32[1,8,64,1024]{3,2,1,0:T(8,128)} %bitcast.106, f32[1,8,64,1024]{3,2,1,0:T(8,128)} %bitcast.125, f32[1,8,64,1024]{3,2,1,0:T(8,128)S(1)} %bitcast.102, f32[1,8,64,1024]{3,2,1,0:T(8,128)} %bitcast.113, ...), kind=kLoop, calls=%fused_computation.56 | loop fusion | flops 34603008 | bytes 18874384 | tf_op jit(solution)/shard_map/concatenate | solution.py:56
  71.4 0.0 copy-done.6
  71.4 8.5 %subtract_multiply_fusion.4 = (f32[8,64,1024]{2,1,0:T(8,128)}, f32[8,64,1024]{2,1,0:T(8,128)S(1)}, f32[8,64,1024]{2,1,0:T(8,128)}, f32[8,64,1024]{2,1,0:T(8,128)}, f32[8,64,1024]{2,1,0:T(8,128)}) fusion(f32[8,64,1024]{2,1,0:T(8,128)S(1)} %bitcast.103, f32[]{:T(128)} %bitcast.5, f32[]{:T(128)} %bitcast.4, f32[]{:T(128)} %bitcast.3, f32[]{:T(128)} %bitcast.1, ...), kind=kLoop, calls=%fused_computation.80 | loop fusion | flops 24641536 | bytes 18874384 | tf_op jit(solution)/shard_map/mul | solution.py:53
  80.0 7.1 %subtract_multiply_fusion.2 = (f32[8,64,1024]{2,1,0:T(8,128)}, f32[8,64,1024]{2,1,0:T(8,128)S(1)}, f32[8,64,1024]{2,1,0:T(8,128)}) fusion(f32[8,64,1024]{2,1,0:T(8,128)S(1)} %bitcast.107, f32[]{:T(128)} %bitcast.5, f32[]{:T(128)} %bitcast.4, f32[]{:T(128)} %bitcast.3, f32[]{:T(128)} %bitcast.1, f32[8,64,1024]{2,1,0:T(8,128)S(1)} %bitcast.126, ...), kind=kLoop, calls=%fused_computation.70 | loop fusion | flops 17825792 | bytes 14680080 | tf_op jit(solution)/shard_map/mul | solution.py:53
  87.0 6.6 %subtract_multiply_fusion.1 = (f32[8,64,1024]{2,1,0:T(8,128)}, f32[8,64,1024]{2,1,0:T(8,128)}) fusion(f32[8,64,1024]{2,1,0:T(8,128)S(1)} %bitcast.123, f32[]{:T(128)} %bitcast.5, f32[]{:T(128)} %bitcast.4, f32[]{:T(128)} %bitcast.3, f32[]{:T(128)} %bitcast.1, f32[8,64,1024]{2,1,0:T(8,128)S(1)} %get-tuple-element.8, f32[8,64,1024]{2,1,0:T(8,128)S(1)} %bitcast.108, ...), kind=kLoop, calls=%fused_computation.65 | loop fusion | flops 17825792 | bytes 12582928 | tf_op jit(solution)/shard_map/mul | solution.py:53
  93.7 0.0 copy-done.15
  93.7 21.7 %maximum_multiply_fusion = f32[1,4,8,64,1024]{4,3,1,2,0:T(8,128)S(1)} fusion(f32[1,1,8,64,1024]{4,3,1,2,0:T(8,128)} %fusion.42, f32[]{:T(128)} %bitcast.35, f32[1,8,64,1024]{3,2,1,0:T(8,128)} %get-tuple-element.52, f32[1,8,64,1024]{3,2,1,0:T(8,128)} %get-tuple-element.53, f32[1,8,64,1024]{3,2,1,0:T(8,128)S(1)} %copy-done.15, ...), kind=kLoop, calls=%fused_computation.2 | loop fusion | flops 90701824 | bytes 77594624 | tf_op jit(solution)/shard_map/mul | solution.py:56
  115.3 3.1 %dynamic-slice_bitcast_fusion = (f32[1,1,4,64,1024]{4,3,2,1,0:T(8,128)}, f32[1,1,4,64,1024]{4,3,2,1,0:T(8,128)}, f32[1,1,4,64,1024]{4,3,2,1,0:T(8,128)}, f32[1,1...) fusion(f32[1,4,8,64,1024]{4,3,1,2,0:T(8,128)S(1)} %maximum_mult, ...), kind=kLoop, calls=%fused_computation.114 | loop fusion | bytes 14680092 | tf_op jit(solution)/shard_map/jit(dynamic_index_in_dim)/dynamic_slice | solution.py:26
  118.4 0.0 collective-permute-start
  118.4 1.5 collective-permute-start.1
  119.9 1.2 collective-permute-start.2
  121.1 1.7 collective-permute-start.3
  122.8 0.0 collective-permute-start.4
  122.8 24.5 %fusion.64 = f32[8,4,64,1024]{3,2,1,0:T(8,128)} fusion(f32[]{:T(128)} %bitcast.35, f32[1,1,8,64,1024]{4,3,1,2,0:T(8,128)} %fusion.42, f32[1,8,64,1024]{3,2,1,0:T(8,128)} %get-tuple-element.52, f32[1,8,64,1024]{3,2,1,0:T(8,128)} %get-tuple-element.53, f32[1,8,64,1024]{3,2,1,0:T(8,128)S(1)} %copy-done.15, f32[1,8,64,1024]{3,2,1,0:T(8,128)} %get-tuple-element.71, ...), kind=kLoop, calls=%fused_computation.152 | loop fusion | flops 90701824 | bytes 77594624 | tf_op jit(solution)/shard_map/reshape | solution.py:17
  147.6 0.1 select_reduce_fusion
  147.7 0.0 collective-permute-done
  147.7 0.6 collective-permute-start.5
  148.3 2.3 bitcast_dynamic-update-slice_fusion.6
  150.6 0.0 collective-permute-done.1
  150.6 0.0 copy-done.16
  150.6 15.4 %collective-permute-start.6 = (f32[1,1,4,64,1024]{4,3,2,1,0:T(8,128)S(1)}, f32[1,1,4,64,1024]{4,3,2,1,0:T(8,128)S(1)}, u32[]{:S(2)}, u32[]{:S(2)}) collective-permute-start(f32[1,1,4,64,1024]{4,3,2,1,0:T(8,128)S(1)} %copy-done.16), channel_id=1, source_target_pairs={{0,7},{1,0},{2,1},{3,2},{4,3},{5,4},{6,5},{7,6},{8,15},{9,8},{10,9... | collective-permute-start | bytes 3145736 | tf_op jit(solution)/shard_map/ppermute | solution.py:27
  166.0 2.3 bitcast_dynamic-update-slice_fusion.5
  168.3 0.0 collective-permute-done.2
  168.3 2.4 bitcast_dynamic-update-slice_fusion.4
  170.7 0.0 collective-permute-done.3
  170.7 2.3 bitcast_dynamic-update-slice_fusion.3
  173.0 38.8 %collective-permute-done.4 = f32[1,1,4,64,1024]{4,3,2,1,0:T(8,128)} collective-permute-done((f32[1,1,4,64,1024]{4,3,2,1,0:T(8,128)}, f32[1,1,4,64,1024]{4,3,2,1,0:T(8,128)}, u32[]{:S(2)}, u32[]{:S(2)}) %collective-permute-start.4) | collective-permute-done | bytes 1048608 | tf_op jit(solution)/shard_map/ppermute | solution.py:27
  211.8 2.3 bitcast_dynamic-update-slice_fusion.2
  214.1 0.0 collective-permute-done.5
  214.1 1.1 bitcast_dynamic-update-slice_fusion.1
  215.3 0.0 collective-permute-done.6
  215.3 1.1 bitcast_dynamic-update-slice_fusion
  216.3 7.7 %gather_fusion = f32[8,4,64,1024]{3,2,1,0:T(8,128)} fusion(f32[8,4,64,1024]{3,2,1,0:T(8,128)} %bitcast_dynamic-update-slice_fusion, s32[1024]{0:T(1024)S(1)} %pad_clamp_fusion.1), kind=kCustom, calls=%fused_computation | custom fusion | bytes 16777248 | tf_op jit(solution)/shard_map/jit(_take)/gather | solution.py:65
  224.0 4.4 %broadcast_select_fusion = f32[8,4,64,1024]{3,2,1,0:T(8,128)S(1)} fusion(f32[8,4,64,1024]{3,2,1,0:T(8,128)} %gather_fusion, pred[8]{0:T(512)(128)(4,1)S(1)} %compare_and_fusion), kind=kLoop, calls=%fused_computation.52 | loop fusion | flops 2097152 | bytes 16777224 | tf_op jit(solution)/shard_map/jit(_take)/select_n | solution.py:65
  228.5 0.5 slice.148
  229.0 0.1 fusion.50
  229.1 1.1 multiply_add_fusion
  230.2 0.1 slice.151
  230.4 0.7 multiply_add_fusion.1
  231.2 0.2 fusion.49
  231.4 1.1 copy.14
  232.5 0.0 copy-start.18
  232.5 2.9 %reshape.2203 = f32[4,1,65536]{2,1,0:T(1,128)} reshape(f32[1024,1,4,64]{3,2,1,0:T(4,128)S(1)} %bitcast.127) | data formatting | bytes 2097152
  235.5 4.9 %all-to-all-start = ((f32[4,1,65536]{2,1,0:T(1,128)}), f32[4,1,65536]{2,1,0:T(1,128)S(1)}, u32[]{:S(2)}, u32[]{:S(2)}) async-start(f32[4,1,65536]{2,1,0:T(1,128)} %reshape.2203), calls=%async_computation | async-start | bytes 2097152 | tf_op jit(solution)/shard_map/all_to_all | solution.py:86
  240.3 0.1 select_reduce_fusion.1
  240.4 26.9 %all-to-all-done = f32[4,1,65536]{2,1,0:T(1,128)S(1)} async-done(((f32[4,1,65536]{2,1,0:T(1,128)}), f32[4,1,65536]{2,1,0:T(1,128)S(1)}, u32[]{:S(2)}, u32[]{:S(2)}) %all-to-all-start) | async-done | bytes 1048608 | tf_op jit(solution)/shard_map/all_to_all | solution.py:86
  267.3 0.5 broadcast.2377
  267.8 3.8 %reduce = f32[4,65536]{1,0:T(4,128)S(1)} reduce(f32[4,1,65536]{2,1,0:T(1,128)S(1)} %all-to-all-done, f32[]{:T(128)} %broadcast.2377), dimensions={1}, to_apply=%all_to_all.13.reduce_sub_computation | reduce | bytes 2097156 | tf_op jit(solution)/shard_map/all_to_all | solution.py:86
  271.6 1.4 reshape.2204
  273.0 0.8 copy.16
  273.9 0.6 gather_fusion.1
  274.5 0.2 broadcast_select_fusion.1
  274.7 0.1 multiply_add_fusion.26
  274.8 0.7 fusion.53
  (42 shorter events, 0.2 us)
Async XLA Ops:
  0.0 147.5 %copy-start = (s32[4,8]{1,0:T(4,128)S(1)}, s32[4,8]{1,0:T(4,128)}, u32[]{:S(2)}) copy-start(s32[4,8]{1,0:T(4,128)} %param.8) | copy-start | bytes 388
  0.7 6.7 %copy-start.17 = (f32[4,4]{1,0:T(4,128)S(1)}, f32[4,4]{1,0:T(4,128)}, u32[]{:S(2)}) copy-start(f32[4,4]{1,0:T(4,128)} %param.6) | copy-start | bytes 196
  7.4 13.9 %copy-start.9 = (f32[1,1,1,512,1024]{4,3,2,1,0:T(8,128)}, f32[1,1,1,512,1024]{4,3,2,1,0:T(8,128)S(1)}, u32[]{:S(2)}) copy-start(f32[1,1,1,512,1024]{4,3,2,1,0:T(8,128)S(1)} %get-tuple-element.15) | copy-start | bytes 6291460
  7.4 13.9 %copy-start.11 = (f32[1,1,1,512,1024]{4,3,2,1,0:T(8,128)}, f32[1,1,1,512,1024]{4,3,2,1,0:T(8,128)S(1)}, u32[]{:S(2)}) copy-start(f32[1,1,1,512,1024]{4,3,2,1,0:T(8,128)S(1)} %get-tuple-element.16) | copy-start | bytes 6291460
  7.4 13.9 %copy-start.1 = (f32[1,1,1,512,1024]{4,3,2,1,0:T(8,128)}, f32[1,1,1,512,1024]{4,3,2,1,0:T(8,128)S(1)}, u32[]{:S(2)}) copy-start(f32[1,1,1,512,1024]{4,3,2,1,0:T(8,128)S(1)} %get-tuple-element.10) | copy-start | bytes 6291460
  7.4 13.9 %copy-start.13 = (f32[1,1,1,512,1024]{4,3,2,1,0:T(8,128)}, f32[1,1,1,512,1024]{4,3,2,1,0:T(8,128)S(1)}, u32[]{:S(2)}) copy-start(f32[1,1,1,512,1024]{4,3,2,1,0:T(8,128)S(1)} %get-tuple-element.11) | copy-start | bytes 6291460
  7.4 26.6 %copy-start.5 = (f32[1,1,1,512,1024]{4,3,2,1,0:T(8,128)}, f32[1,1,1,512,1024]{4,3,2,1,0:T(8,128)S(1)}, u32[]{:S(2)}) copy-start(f32[1,1,1,512,1024]{4,3,2,1,0:T(8,128)S(1)} %get-tuple-element.13) | copy-start | bytes 6291460
  7.5 39.4 %copy-start.3 = (f32[1,1,1,512,1024]{4,3,2,1,0:T(8,128)}, f32[1,1,1,512,1024]{4,3,2,1,0:T(8,128)S(1)}, u32[]{:S(2)}) copy-start(f32[1,1,1,512,1024]{4,3,2,1,0:T(8,128)S(1)} %get-tuple-element.9) | copy-start | bytes 6291460
  7.5 39.4 %copy-start.7 = (f32[1,1,1,512,1024]{4,3,2,1,0:T(8,128)}, f32[1,1,1,512,1024]{4,3,2,1,0:T(8,128)S(1)}, u32[]{:S(2)}) copy-start(f32[1,1,1,512,1024]{4,3,2,1,0:T(8,128)S(1)} %get-tuple-element.14) | copy-start | bytes 6291460
  59.6 11.8 %copy-start.4 = (f32[1,1,1,512,1024]{4,3,2,1,0:T(8,128)S(1)}, f32[1,1,1,512,1024]{4,3,2,1,0:T(8,128)}, u32[]{:S(2)}) copy-start(f32[1,1,1,512,1024]{4,3,2,1,0:T(8,128)} %copy-done.3) | copy-start | bytes 6291460
  59.6 11.8 %copy-start.6 = (f32[1,1,1,512,1024]{4,3,2,1,0:T(8,128)S(1)}, f32[1,1,1,512,1024]{4,3,2,1,0:T(8,128)}, u32[]{:S(2)}) copy-start(f32[1,1,1,512,1024]{4,3,2,1,0:T(8,128)} %copy-done.5) | copy-start | bytes 6291460
  59.6 11.8 %copy-start.8 = (f32[1,1,1,512,1024]{4,3,2,1,0:T(8,128)S(1)}, f32[1,1,1,512,1024]{4,3,2,1,0:T(8,128)}, u32[]{:S(2)}) copy-start(f32[1,1,1,512,1024]{4,3,2,1,0:T(8,128)} %copy-done.7) | copy-start | bytes 6291460
  71.4 8.5 %copy-start.2 = (f32[1,1,1,512,1024]{4,3,2,1,0:T(8,128)S(1)}, f32[1,1,1,512,1024]{4,3,2,1,0:T(8,128)}, u32[]{:S(2)}) copy-start(f32[1,1,1,512,1024]{4,3,2,1,0:T(8,128)} %copy-done.1) | copy-start | bytes 6291460
  71.4 8.5 %copy-start.14 = (f32[1,1,1,512,1024]{4,3,2,1,0:T(8,128)S(1)}, f32[1,1,1,512,1024]{4,3,2,1,0:T(8,128)}, u32[]{:S(2)}) copy-start(f32[1,1,1,512,1024]{4,3,2,1,0:T(8,128)} %copy-done.13) | copy-start | bytes 6291460
  79.9 7.1 %copy-start.10 = (f32[1,1,1,512,1024]{4,3,2,1,0:T(8,128)S(1)}, f32[1,1,1,512,1024]{4,3,2,1,0:T(8,128)}, u32[]{:S(2)}) copy-start(f32[1,1,1,512,1024]{4,3,2,1,0:T(8,128)} %copy-done.9) | copy-start | bytes 6291460
  79.9 7.1 %copy-start.12 = (f32[1,1,1,512,1024]{4,3,2,1,0:T(8,128)S(1)}, f32[1,1,1,512,1024]{4,3,2,1,0:T(8,128)}, u32[]{:S(2)}) copy-start(f32[1,1,1,512,1024]{4,3,2,1,0:T(8,128)} %copy-done.11) | copy-start | bytes 6291460
  87.0 6.6 %copy-start.15 = (f32[1,8,64,1024]{3,2,1,0:T(8,128)S(1)}, f32[1,8,64,1024]{3,2,1,0:T(8,128)}, u32[]{:S(2)}) copy-start(f32[1,8,64,1024]{3,2,1,0:T(8,128)} %get-tuple-element.51) | copy-start | bytes 6291460
  118.4 29.3 %collective-permute-start = (f32[1,1,4,64,1024]{4,3,2,1,0:T(8,128)}, f32[1,1,4,64,1024]{4,3,2,1,0:T(8,128)}, u32[]{:S(2)}, u32[]{:S(2)}) collective-permute-start(f32[1,1,4,64,1024]{4,3,2,1,0:T(8,128)} %get-tuple-element.23), channel_id=1, source_target_pairs={{0,1},{1,2},{2,3},{3,4},{4,5},{5,6},{6,7},{7,0},{8,9},{9,10},{10,1... | collective-permute-start | bytes 3145736 | tf_op jit(solution)/shard_map/ppermute | solution.py:27
  118.4 32.2 %collective-permute-start.1 = (f32[1,1,4,64,1024]{4,3,2,1,0:T(8,128)}, f32[1,1,4,64,1024]{4,3,2,1,0:T(8,128)}, u32[]{:S(2)}, u32[]{:S(2)}) collective-permute-start(f32[1,1,4,64,1024]{4,3,2,1,0:T(8,128)} %get-tuple-element.22), channel_id=1, source_target_pairs={{0,2},{1,3},{2,4},{3,5},{4,6},{5,7},{6,0},{7,1},{8,10},{9,11},{10,... | collective-permute-start | bytes 3145736 | tf_op jit(solution)/shard_map/ppermute | solution.py:27
  119.9 48.4 %collective-permute-start.2 = (f32[1,1,4,64,1024]{4,3,2,1,0:T(8,128)}, f32[1,1,4,64,1024]{4,3,2,1,0:T(8,128)}, u32[]{:S(2)}, u32[]{:S(2)}) collective-permute-start(f32[1,1,4,64,1024]{4,3,2,1,0:T(8,128)} %get-tuple-element.21), channel_id=1, source_target_pairs={{0,3},{1,4},{2,5},{3,6},{4,7},{5,0},{6,1},{7,2},{8,11},{9,12},{10,... | collective-permute-start | bytes 3145736 | tf_op jit(solution)/shard_map/ppermute | solution.py:27
  121.1 49.6 %collective-permute-start.3 = (f32[1,1,4,64,1024]{4,3,2,1,0:T(8,128)}, f32[1,1,4,64,1024]{4,3,2,1,0:T(8,128)}, u32[]{:S(2)}, u32[]{:S(2)}) collective-permute-start(f32[1,1,4,64,1024]{4,3,2,1,0:T(8,128)} %get-tuple-element.20), channel_id=1, source_target_pairs={{0,4},{1,5},{2,6},{3,7},{4,0},{5,1},{6,2},{7,3},{8,12},{9,13},{10,... | collective-permute-start | bytes 3145736 | tf_op jit(solution)/shard_map/ppermute | solution.py:27
  122.8 89.0 %collective-permute-start.4 = (f32[1,1,4,64,1024]{4,3,2,1,0:T(8,128)}, f32[1,1,4,64,1024]{4,3,2,1,0:T(8,128)}, u32[]{:S(2)}, u32[]{:S(2)}) collective-permute-start(f32[1,1,4,64,1024]{4,3,2,1,0:T(8,128)} %get-tuple-element.19), channel_id=1, source_target_pairs={{0,5},{1,6},{2,7},{3,0},{4,1},{5,2},{6,3},{7,4},{8,13},{9,14},{10,... | collective-permute-start | bytes 3145736 | tf_op jit(solution)/shard_map/ppermute | solution.py:27
  147.4 3.2 %copy-start.16 = (f32[1,1,4,64,1024]{4,3,2,1,0:T(8,128)S(1)}, f32[1,1,4,64,1024]{4,3,2,1,0:T(8,128)}, u32[]{:S(2)}) copy-start(f32[1,1,4,64,1024]{4,3,2,1,0:T(8,128)} %get-tuple-element.17) | copy-start | bytes 3145732
  147.7 66.5 %collective-permute-start.5 = (f32[1,1,4,64,1024]{4,3,2,1,0:T(8,128)}, f32[1,1,4,64,1024]{4,3,2,1,0:T(8,128)S(1)}, u32[]{:S(2)}, u32[]{:S(2)}) collective-permute-start(f32[1,1,4,64,1024]{4,3,2,1,0:T(8,128)} %get-tuple-element.18), channel_id=1, source_target_pairs={{0,6},{1,7},{2,0},{3,1},{4,2},{5,3},{6,4},{7,5},{8,14},{9,15},{10,... | collective-permute-start | bytes 3145736 | tf_op jit(solution)/shard_map/ppermute | solution.py:27
  150.6 64.6 %collective-permute-start.6 = (f32[1,1,4,64,1024]{4,3,2,1,0:T(8,128)S(1)}, f32[1,1,4,64,1024]{4,3,2,1,0:T(8,128)S(1)}, u32[]{:S(2)}, u32[]{:S(2)}) collective-permute-start(f32[1,1,4,64,1024]{4,3,2,1,0:T(8,128)S(1)} %copy-done.16), channel_id=1, source_target_pairs={{0,7},{1,0},{2,1},{3,2},{4,3},{5,4},{6,5},{7,6},{8,15},{9,8},{10,9... | collective-permute-start | bytes 3145736 | tf_op jit(solution)/shard_map/ppermute | solution.py:27
  232.5 7.8 %copy-start.18 = (s32[4]{0:T(128)S(1)}, s32[4]{0:T(128)}, u32[]{:S(2)}) copy-start(s32[4]{0:T(128)} %param.7) | copy-start | bytes 52
  235.5 31.9 %all-to-all-start = ((f32[4,1,65536]{2,1,0:T(1,128)}), f32[4,1,65536]{2,1,0:T(1,128)S(1)}, u32[]{:S(2)}, u32[]{:S(2)}) async-start(f32[4,1,65536]{2,1,0:T(1,128)} %reshape.2203), calls=%async_computation | async-start | bytes 2097152 | tf_op jit(solution)/shard_map/all_to_all | solution.py:86
